TPU v7x, 512 devices: a whole 4x8x8 slice. The times are simulated.
512 devices in a mesh: pb: 32 (over x, z), ao: 16 (over y, core).
Axes of the slice: x: 4, y: 8, z: 8, core: 2. Of those that a mesh axis runs over, the one named last changes fastest.
Arguments:
- queries: bfloat16 [32768, 128], P('pb'), may hold values from -4 to 4
- centres: bfloat16 [32768, 128], P(('pb', 'ao')), may hold values from -4 to 4
- coefs: bfloat16 [32768, 4096], P('pb', 'ao'), may hold values from -3 to 3
- pattern: int32 [32, 5], replicated, may hold values from 0 to 1, as said below
Outputs:
- scores: bfloat16 [32768, 4096], P('pb', 'ao')
Inputs may be any that keep to these rules, and one draw needn't show every extreme that they name: pattern[i, j] tells whether query block i lists centre block i + j - 2; it is 0 where that block lies outside 0 to 31, and 1 for j = 2.
All inputs are finite; a program needn't handle non-finite values.
Results may differ from a plain program's by a relative error of at most 0.0049.
Values may be sent and summed in bfloat16 or wider, within the bound.
A program may use at most 64 MiB of HBM per device.

v0:
```python
import math

import jax
import jax.numpy as jnp
from jax import lax
from jax.sharding import PartitionSpec as P

RADIUS_FACTOR = 1.3


def shifted(block, axis, distance):
    devices = range(lax.axis_size(axis))
    route = [(i - distance, i) for i in devices if i - distance in devices]
    return lax.ppermute(block, axis, route)


def query_norms(query_rows):
    query_wide = query_rows.astype(jnp.float32)
    return jnp.sum(query_wide * query_wide, axis=1)[:, None]


def wendland_block(query_rows, query_norm, centre_rows):
    centre_wide = centre_rows.astype(jnp.float32)
    centre_norm = jnp.sum(centre_wide * centre_wide, axis=1)[None, :]
    cross = jnp.dot(query_rows, centre_rows.T, preferred_element_type=jnp.float32)
    dist = jnp.sqrt(query_norm + centre_norm - 2.0 * cross)
    scaled = dist / (RADIUS_FACTOR * math.sqrt(query_rows.shape[1]))
    inner = jnp.maximum(1.0 - scaled, 0.0)
    return inner * inner * inner * inner * (4.0 * scaled + 1.0)


def contribute(query_rows, query_norm, centre_rows, coef_rows, weight):
    kern = (
        wendland_block(query_rows, query_norm, centre_rows) * weight.astype(jnp.float32)
    ).astype(jnp.bfloat16)
    return jnp.dot(kern, coef_rows, preferred_element_type=jnp.float32)


def per_device(queries, centres, coefs, pattern):
    band_width = pattern.shape[1]
    half_band = band_width // 2
    my_block = lax.axis_index("pb")
    my_pattern = lax.dynamic_index_in_dim(pattern, my_block, 0, keepdims=False)
    panel_coords = lax.all_gather(centres, "ao", axis=0, tiled=True)
    my_norm = query_norms(queries)
    offsets = [shift_by for shift_by in range(-half_band, half_band + 1) if shift_by != 0]
    accumulated = contribute(queries, my_norm, panel_coords, coefs, my_pattern[half_band])
    for shift_by in offsets:
        far_coords, far_coefs = shifted((panel_coords, coefs), "pb", -shift_by)
        accumulated = accumulated + contribute(
            queries, my_norm, far_coords, far_coefs, my_pattern[half_band + shift_by]
        )
    return accumulated.astype(jnp.bfloat16)


def solution(mesh):
    in_specs = (P("pb", None), P(("pb", "ao"), None), P("pb", "ao"), P())
    out_specs = P("pb", "ao")
    return jax.shard_map(
        per_device, mesh=mesh, in_specs=in_specs, out_specs=out_specs, check_vma=False
    )
```

profile of v0, /device:TPU:6, one launch (start us, length us, event | category | flops | bytes accessed | tf_op | source)
XLA Modules:
  0.0 104.0 jit_solution(7479997999850689913)
XLA Ops:
  0.0 0.0 copy-start
  0.0 18.7 %all_gather.3 = bf16[1024,128]{1,0:T(8,128)(2,1)S(1)} all-gather(bf16[64,128]{1,0:T(8,128)(2,1)} %param.5), channel_id=1, replica_groups=mesh['pb'=32,'ao'=16] {'ao'}, dimensions={0}, use_global_device_ids=true | all-gather | bytes 278528 | tf_op jit(solution)/shard_map/all_gather | solution.py:44
  18.7 11.2 %collective-permute-start.6 = (bf16[1024,128]{1,0:T(8,128)(2,1)S(1)}, bf16[1024,128]{1,0:T(8,128)(2,1)S(1)}, u32[]{:S(2)}, u32[]{:S(2)}) collective-permute-start(bf16[1024,128]{1,0:T(8,128)(2,1)S(1)} %all_gather.3), channel_id=1, source_target_pairs={{32,0},{48,16},{64,32},{80,48},{96,64},{112,80},{128,96},{144,112}... | collective-permute-start | bytes 786440 | tf_op jit(solution)/shard_map/ppermute | solution.py:14
  29.9 2.5 %collective-permute-start.4 = (bf16[1024,128]{1,0:T(8,128)(2,1)S(1)}, bf16[1024,128]{1,0:T(8,128)(2,1)S(1)}, u32[]{:S(2)}, u32[]{:S(2)}) collective-permute-start(bf16[1024,128]{1,0:T(8,128)(2,1)S(1)} %all_gather.3), channel_id=1, source_target_pairs={{16,0},{32,16},{48,32},{64,48},{80,64},{96,80},{112,96},{128,112},... | collective-permute-start | bytes 786440 | tf_op jit(solution)/shard_map/ppermute | solution.py:14
  32.3 3.4 %collective-permute-start.2 = (bf16[1024,128]{1,0:T(8,128)(2,1)S(1)}, bf16[1024,128]{1,0:T(8,128)(2,1)S(1)}, u32[]{:S(2)}, u32[]{:S(2)}) collective-permute-start(bf16[1024,128]{1,0:T(8,128)(2,1)S(1)} %all_gather.3), channel_id=1, source_target_pairs={{0,16},{16,32},{32,48},{48,64},{64,80},{80,96},{96,112},{112,128},... | collective-permute-start | bytes 786440 | tf_op jit(solution)/shard_map/ppermute | solution.py:14
  35.7 2.8 %collective-permute-start = (bf16[1024,128]{1,0:T(8,128)(2,1)S(1)}, bf16[1024,128]{1,0:T(8,128)(2,1)S(1)}, u32[]{:S(2)}, u32[]{:S(2)}) collective-permute-start(bf16[1024,128]{1,0:T(8,128)(2,1)S(1)} %all_gather.3), channel_id=1, source_target_pairs={{0,32},{16,48},{32,64},{48,80},{64,96},{80,112},{96,128},{112,144}... | collective-permute-start | bytes 786440 | tf_op jit(solution)/shard_map/ppermute | solution.py:14
  38.6 2.5 %collective-permute-start.3 = (bf16[1024,256]{1,0:T(8,128)(2,1)}, bf16[1024,256]{1,0:T(8,128)(2,1)S(1)}, u32[]{:S(2)}, u32[]{:S(2)}) collective-permute-start(bf16[1024,256]{1,0:T(8,128)(2,1)} %param.6), channel_id=1, source_target_pairs={{0,16},{16,32},{32,48},{48,64},{64,80},{80,96},{96,112},{112,128},... | collective-permute-start | bytes 1572872 | tf_op jit(solution)/shard_map/ppermute | solution.py:14
  41.0 0.2 multiply_reduce_fusion.4
  41.3 0.1 constant_dynamic-slice_fusion
  41.3 0.6 fusion.50
  42.7 1.2 %multiply_reduce_fusion.5 = f32[1024]{0:T(1024)S(1)} fusion(bf16[1024,128]{1,0:T(8,128)(2,1)} %param.4), kind=kLoop, calls=%fused_computation.35 | loop fusion | flops 392192 | bytes 266240 | tf_op jit(solution)/shard_map/reduce_sum | solution.py:19
  43.8 0.0 copy-start.2
  43.8 5.2 %fusion.19 = f32[1024,256]{1,0:T(8,128)} fusion(bf16[1024,256]{1,0:T(8,128)(2,1)} %param.6, bf16[1024,128]{1,0:T(8,128)(2,1)} %param.4, bf16[1024,128]{1,0:T(8,128)(2,1)S(1)} %all_gather.3, f32[]{:T(128)} %bitcast, f32[1024]{0:T(1024)S(1)} %multiply_reduce_fusion.4, f32[1024]{0:T(1024)S(1)} %multiply_reduce_fusion.5), kind=kOutput, calls=%fused_computation.24 | convolution fusion | flops 819986432 | bytes 2105348 | tf_op jit(solution)/shard_map/dot_general | solution.py:36
  51.7 0.0 collective-permute-done.6
  51.7 2.2 %collective-permute-start.1 = (bf16[1024,256]{1,0:T(8,128)(2,1)S(1)}, bf16[1024,256]{1,0:T(8,128)(2,1)S(1)}, u32[]{:S(2)}, u32[]{:S(2)}) collective-permute-start(bf16[1024,256]{1,0:T(8,128)(2,1)S(1)} %copy-done.2), channel_id=1, source_target_pairs={{0,32},{16,48},{32,64},{48,80},{64,96},{80,112},{96,128},{112,144}... | collective-permute-start | bytes 1572872 | tf_op jit(solution)/shard_map/ppermute | solution.py:14
  53.9 0.2 multiply_reduce_fusion
  54.1 0.0 collective-permute-done.4
  54.1 6.7 %collective-permute-start.7 = (bf16[1024,256]{1,0:T(8,128)(2,1)S(1)}, bf16[1024,256]{1,0:T(8,128)(2,1)}, u32[]{:S(2)}, u32[]{:S(2)}) collective-permute-start(bf16[1024,256]{1,0:T(8,128)(2,1)S(1)} %copy-done.2), channel_id=1, source_target_pairs={{32,0},{48,16},{64,32},{80,48},{96,64},{112,80},{128,96},{144,112}... | collective-permute-start | bytes 1572872 | tf_op jit(solution)/shard_map/ppermute | solution.py:14
  60.8 0.2 multiply_reduce_fusion.1
  61.0 0.0 collective-permute-done.2
  61.0 3.6 %collective-permute-start.5 = (bf16[1024,256]{1,0:T(8,128)(2,1)S(1)}, bf16[1024,256]{1,0:T(8,128)(2,1)}, u32[]{:S(2)}, u32[]{:S(2)}) collective-permute-start(bf16[1024,256]{1,0:T(8,128)(2,1)S(1)} %copy-done.2), channel_id=1, source_target_pairs={{16,0},{32,16},{48,32},{64,48},{80,64},{96,80},{112,96},{128,112},... | collective-permute-start | bytes 1572872 | tf_op jit(solution)/shard_map/ppermute | solution.py:14
  64.6 0.2 multiply_reduce_fusion.2
  64.8 0.0 collective-permute-done
  64.8 0.2 multiply_reduce_fusion.3
  65.0 3.8 %collective-permute-done.3 = bf16[1024,256]{1,0:T(8,128)(2,1)S(1)} collective-permute-done((bf16[1024,256]{1,0:T(8,128)(2,1)}, bf16[1024,256]{1,0:T(8,128)(2,1)S(1)}, u32[]{:S(2)}, u32[]{:S(2)}) %collective-permute-start.3) | collective-permute-done | bytes 524320 | tf_op jit(solution)/shard_map/ppermute | solution.py:14
  68.9 4.1 %fusion.17 = f32[1024,256]{1,0:T(8,128)} fusion(bf16[1024,256]{1,0:T(8,128)(2,1)S(1)} %collective-permute-done.3, bf16[1024,128]{1,0:T(8,128)(2,1)S(1)} %copy-done.1, bf16[1024,128]{1,0:T(8,128)(2,1)S(1)} %collective-permute-done.2, f32[]{:T(128)} %bitcast.2, f32[1024]{0:T(1024)S(1)} %multiply_reduce_fusion.2, f32[1024]{0:T(1024)S(1)} %multiply_reduce_fusion.5), kind=kOutput, calls=%fused_computation.22 | convolution fusion | flops 819986432 | bytes 2105348 | tf_op jit(solution)/shard_map/dot_general | solution.py:36
  73.0 8.4 %collective-permute-done.7 = bf16[1024,256]{1,0:T(8,128)(2,1)} collective-permute-done((bf16[1024,256]{1,0:T(8,128)(2,1)S(1)}, bf16[1024,256]{1,0:T(8,128)(2,1)}, u32[]{:S(2)}, u32[]{:S(2)}) %collective-permute-start.7) | collective-permute-done | bytes 524320 | tf_op jit(solution)/shard_map/ppermute | solution.py:14
  81.4 5.1 %fusion.15 = f32[1024,256]{1,0:T(8,128)} fusion(bf16[1024,256]{1,0:T(8,128)(2,1)} %collective-permute-done.7, bf16[1024,128]{1,0:T(8,128)(2,1)S(1)} %copy-done.1, bf16[1024,128]{1,0:T(8,128)(2,1)S(1)} %collective-permute-done.6, f32[]{:T(128)} %bitcast.4, f32[1024]{0:T(1024)S(1)} %multiply_reduce_fusion, f32[1024]{0:T(1024)S(1)} %multiply_reduce_fusion.5), kind=kOutput, calls=%fused_computation.20 | convolution fusion | flops 819986432 | bytes 2105348 | tf_op jit(solution)/shard_map/dot_general | solution.py:36
  86.5 6.8 %collective-permute-done.5 = bf16[1024,256]{1,0:T(8,128)(2,1)} collective-permute-done((bf16[1024,256]{1,0:T(8,128)(2,1)S(1)}, bf16[1024,256]{1,0:T(8,128)(2,1)}, u32[]{:S(2)}, u32[]{:S(2)}) %collective-permute-start.5) | collective-permute-done | bytes 524320 | tf_op jit(solution)/shard_map/ppermute | solution.py:14
  93.3 5.1 %fusion.16 = f32[1024,256]{1,0:T(8,128)} fusion(bf16[1024,256]{1,0:T(8,128)(2,1)} %collective-permute-done.5, bf16[1024,128]{1,0:T(8,128)(2,1)S(1)} %copy-done.1, bf16[1024,128]{1,0:T(8,128)(2,1)S(1)} %collective-permute-done.4, f32[]{:T(128)} %bitcast.3, f32[1024]{0:T(1024)S(1)} %multiply_reduce_fusion.1, f32[1024]{0:T(1024)S(1)} %multiply_reduce_fusion.5), kind=kOutput, calls=%fused_computation.21 | convolution fusion | flops 819986432 | bytes 2105348 | tf_op jit(solution)/shard_map/dot_general | solution.py:36
  98.4 0.0 collective-permute-done.1
  98.4 5.6 %fusion.24 = bf16[1024,256]{1,0:T(8,128)(2,1)} fusion(f32[1024,256]{1,0:T(8,128)} %fusion.15, f32[1024,256]{1,0:T(8,128)} %fusion.16, f32[1024,256]{1,0:T(8,128)} %fusion.17, f32[1024,256]{1,0:T(8,128)} %fusion.19, bf16[1024,256]{1,0:T(8,128)(2,1)S(1)} %collective-permute-done.1, bf16[1024,128]{1,0:T(8,128)(2,1)S(1)} %copy-done.1, ...), kind=kOutput, calls=%fused_computation.29 | convolution fusion | flops 821297152 | bytes 5775364 | tf_op jit(solution)/shard_map/dot_general | solution.py:36
  (4 shorter events, 0.0 us)
Async XLA Ops:
  0.0 41.3 %copy-start = (s32[32,5]{0,1:T(8,128)S(1)}, s32[32,5]{0,1:T(8,128)}, u32[]{:S(2)}) copy-start(s32[32,5]{0,1:T(8,128)} %param.7) | copy-start | bytes 1924
  18.7 33.0 %collective-permute-start.6 = (bf16[1024,128]{1,0:T(8,128)(2,1)S(1)}, bf16[1024,128]{1,0:T(8,128)(2,1)S(1)}, u32[]{:S(2)}, u32[]{:S(2)}) collective-permute-start(bf16[1024,128]{1,0:T(8,128)(2,1)S(1)} %all_gather.3), channel_id=1, source_target_pairs={{32,0},{48,16},{64,32},{80,48},{96,64},{112,80},{128,96},{144,112}... | collective-permute-start | bytes 786440 | tf_op jit(solution)/shard_map/ppermute | solution.py:14
  29.9 24.3 %collective-permute-start.4 = (bf16[1024,128]{1,0:T(8,128)(2,1)S(1)}, bf16[1024,128]{1,0:T(8,128)(2,1)S(1)}, u32[]{:S(2)}, u32[]{:S(2)}) collective-permute-start(bf16[1024,128]{1,0:T(8,128)(2,1)S(1)} %all_gather.3), channel_id=1, source_target_pairs={{16,0},{32,16},{48,32},{64,48},{80,64},{96,80},{112,96},{128,112},... | collective-permute-start | bytes 786440 | tf_op jit(solution)/shard_map/ppermute | solution.py:14
  32.3 28.7 %collective-permute-start.2 = (bf16[1024,128]{1,0:T(8,128)(2,1)S(1)}, bf16[1024,128]{1,0:T(8,128)(2,1)S(1)}, u32[]{:S(2)}, u32[]{:S(2)}) collective-permute-start(bf16[1024,128]{1,0:T(8,128)(2,1)S(1)} %all_gather.3), channel_id=1, source_target_pairs={{0,16},{16,32},{32,48},{48,64},{64,80},{80,96},{96,112},{112,128},... | collective-permute-start | bytes 786440 | tf_op jit(solution)/shard_map/ppermute | solution.py:14
  35.7 29.1 %collective-permute-start = (bf16[1024,128]{1,0:T(8,128)(2,1)S(1)}, bf16[1024,128]{1,0:T(8,128)(2,1)S(1)}, u32[]{:S(2)}, u32[]{:S(2)}) collective-permute-start(bf16[1024,128]{1,0:T(8,128)(2,1)S(1)} %all_gather.3), channel_id=1, source_target_pairs={{0,32},{16,48},{32,64},{48,80},{64,96},{80,112},{96,128},{112,144}... | collective-permute-start | bytes 786440 | tf_op jit(solution)/shard_map/ppermute | solution.py:14
  38.6 30.3 %collective-permute-start.3 = (bf16[1024,256]{1,0:T(8,128)(2,1)}, bf16[1024,256]{1,0:T(8,128)(2,1)S(1)}, u32[]{:S(2)}, u32[]{:S(2)}) collective-permute-start(bf16[1024,256]{1,0:T(8,128)(2,1)} %param.6), channel_id=1, source_target_pairs={{0,16},{16,32},{32,48},{48,64},{64,80},{80,96},{96,112},{112,128},... | collective-permute-start | bytes 1572872 | tf_op jit(solution)/shard_map/ppermute | solution.py:14
  43.8 7.9 %copy-start.2 = (bf16[1024,256]{1,0:T(8,128)(2,1)S(1)}, bf16[1024,256]{1,0:T(8,128)(2,1)}, u32[]{:S(2)}) copy-start(bf16[1024,256]{1,0:T(8,128)(2,1)} %param.6) | copy-start | bytes 1572868
  49.1 19.8 %copy-start.1 = (bf16[1024,128]{1,0:T(8,128)(2,1)S(1)}, bf16[1024,128]{1,0:T(8,128)(2,1)}, u32[]{:S(2)}) copy-start(bf16[1024,128]{1,0:T(8,128)(2,1)} %param.4) | copy-start | bytes 786436
  51.7 46.7 %collective-permute-start.1 = (bf16[1024,256]{1,0:T(8,128)(2,1)S(1)}, bf16[1024,256]{1,0:T(8,128)(2,1)S(1)}, u32[]{:S(2)}, u32[]{:S(2)}) collective-permute-start(bf16[1024,256]{1,0:T(8,128)(2,1)S(1)} %copy-done.2), channel_id=1, source_target_pairs={{0,32},{16,48},{32,64},{48,80},{64,96},{80,112},{96,128},{112,144}... | collective-permute-start | bytes 1572872 | tf_op jit(solution)/shard_map/ppermute | solution.py:14
  54.1 27.2 %collective-permute-start.7 = (bf16[1024,256]{1,0:T(8,128)(2,1)S(1)}, bf16[1024,256]{1,0:T(8,128)(2,1)}, u32[]{:S(2)}, u32[]{:S(2)}) collective-permute-start(bf16[1024,256]{1,0:T(8,128)(2,1)S(1)} %copy-done.2), channel_id=1, source_target_pairs={{32,0},{48,16},{64,32},{80,48},{96,64},{112,80},{128,96},{144,112}... | collective-permute-start | bytes 1572872 | tf_op jit(solution)/shard_map/ppermute | solution.py:14
  61.0 32.2 %collective-permute-start.5 = (bf16[1024,256]{1,0:T(8,128)(2,1)S(1)}, bf16[1024,256]{1,0:T(8,128)(2,1)}, u32[]{:S(2)}, u32[]{:S(2)}) collective-permute-start(bf16[1024,256]{1,0:T(8,128)(2,1)S(1)} %copy-done.2), channel_id=1, source_target_pairs={{16,0},{32,16},{48,32},{64,48},{80,64},{96,80},{112,96},{128,112},... | collective-permute-start | bytes 1572872 | tf_op jit(solution)/shard_map/ppermute | solution.py:14
where the time goes:
time: 105 us; the launch traced here: 104 us
  starting transfers between devices  34.7 us (33%)
  matrix products  25.1 us (24%)
  waiting for transfers between devices  19.1 us (18%)
  blocking collectives  18.7 us (18%)
  between operations  3.51 us (3%)
  other arithmetic  2.2 us (2%)
    ppermute x8, starting transfers between devices, shifted(): return lax.ppermute(block, axis, route)  34.7 us
    dot_general x5, matrix products, contribute(): return jnp.dot(kern, coef_rows, preferred_element_type=jnp.float32)  25.1 us
    ppermute x8, waiting for transfers between devices, shifted(): return lax.ppermute(block, axis, route)  19.1 us
    all_gather x1, blocking collectives, per_device(): panel_coords = lax.all_gather(centres, 'ao', axis=0, tiled=True)  18.7 us
  transfers between devices with their start and end apart: 8, of which 3 were waited for; matrix products, arithmetic and copies ran while one was open for 22% of the time, Pallas kernels for 0%

commit v1 on v0

v1 whole, which is shorter than its diff:
```python
import functools
import math

import jax
import jax.numpy as jnp
from jax import lax
from jax.experimental import pallas as pl
from jax.experimental.pallas import tpu as pltpu
from jax.sharding import PartitionSpec as P

RADIUS_FACTOR = 1.3
MESH = pl.DeviceIdType.MESH
F32 = jnp.float32
BF16 = jnp.bfloat16

OFFSETS = (0, -1, 1, -2, 2)
GROUPS = ((0, 1), (1, 3), (3, 5))
CHUNKS = 4


def wendland(sq_dist, radius, high, low):
    clamped = jnp.maximum(sq_dist, 1e-30)
    inner = jnp.maximum(radius - clamped * lax.rsqrt(clamped), 0.0)
    square = inner * inner
    return ((square * square) * (high - low * inner)).astype(BF16)


def kernel(
    n_pb, n_ao,
    queries_hbm, centres_hbm, coefs_hbm, pattern_hbm, out_ref,
    queries, wide_queries, ones, centres, coefs, kern, total, pattern,
    local_sem, zs, zr, ys, yr, ss, sr, ks, kr,
):
    n_y = n_ao // 2
    half = n_y // 2
    n_q, features = queries.shape
    rows = centres.shape[2]
    per_y = 2 * rows
    block = n_y * per_y
    chunk = block // CHUNKS
    radius = RADIUS_FACTOR * math.sqrt(features)

    pb = lax.axis_index("pb")
    ao = lax.axis_index("ao")
    y = ao // 2
    core = ao % 2
    sibling = (pb, y * 2 + (1 - core))
    y_up = (pb, lax.rem(y + 1, n_y) * 2 + core)
    y_down = (pb, lax.rem(y + n_y - 1, n_y) * 2 + core)
    pb_up = (lax.rem(pb + 1, n_pb), ao)
    pb_down = (lax.rem(pb + n_pb - 1, n_pb), ao)

    barrier = pltpu.get_barrier_semaphore()
    for peer in (pb_up, pb_down, y_up, y_down, sibling):
        pl.semaphore_signal(barrier, inc=1, device_id=peer, device_id_type=MESH)

    own_centres = pltpu.make_async_copy(centres_hbm, centres.at[ao, 0], local_sem.at[0])
    own_coefs = pltpu.make_async_copy(coefs_hbm, coefs.at[0], local_sem.at[1])
    own_queries = pltpu.make_async_copy(queries_hbm, queries, local_sem.at[2])
    own_pattern = pltpu.make_async_copy(pattern_hbm, pattern, local_sem.at[3])
    own_centres.start()
    own_coefs.start()
    own_queries.start()
    own_pattern.start()
    own_centres.wait()
    own_coefs.wait()
    pl.semaphore_wait(barrier, 5)

    started = []

    def send(src, dst, send_sem, recv_sem, device):
        copy = pltpu.make_async_remote_copy(
            src_ref=src, dst_ref=dst, send_sem=send_sem, recv_sem=recv_sem,
            device_id=device, device_id_type=MESH,
        )
        copy.start()
        started.append(copy)

    def z_copy(direction, hop):
        src = 0 if hop == 0 else 1 + direction
        return (
            centres.at[ao, src], centres.at[ao, 1 + 2 * hop + direction],
            zs.at[direction, hop], zr.at[direction, hop], (pb_up, pb_down)[direction],
        )

    def coef_copy(direction, hop, part):
        src = 0 if hop == 0 else 1 + direction
        span = pl.ds(part * chunk, chunk)
        return (
            coefs.at[src, span], coefs.at[1 + 2 * hop + direction, span],
            ks.at[direction, hop, part], kr.at[direction, hop, part], (pb_up, pb_down)[direction],
        )

    def ring_view(group, owner, of_core):
        first, last = GROUPS[group]
        return centres.at[owner * 2 + of_core, pl.ds(first, last - first)]

    def owner_of(direction, hop):
        return lax.rem(y + n_y - hop, n_y) if direction == 0 else lax.rem(y + hop, n_y)

    def ring_copy(group, direction, hop):
        view = ring_view(group, owner_of(direction, hop), core)
        return (
            view, view, ys.at[group, direction, hop], yr.at[group, direction, hop],
            (y_up, y_down)[direction],
        )

    def sibling_copy(group, direction, hop, of_core):
        view = ring_view(group, owner_of(direction, hop), of_core)
        return (view, view, ss.at[group, direction, hop], sr.at[group, direction, hop], sibling)

    def arrived(args):
        src, dst, send_sem, recv_sem, device = args
        pltpu.make_async_remote_copy(
            src_ref=src, dst_ref=dst, send_sem=send_sem, recv_sem=recv_sem,
            device_id=device, device_id_type=MESH,
        ).wait_recv()

    def ring_arrived(group, direction, hop):
        view = ring_view(group, owner_of(direction, hop), core)
        arrived((view, view, ys.at[group, direction, hop - 1], yr.at[group, direction, hop - 1],
                 (y_up, y_down)[direction]))

    def start_own(group):
        send(*ring_copy(group, 0, 0))
        send(*ring_copy(group, 1, 0))
        send(*sibling_copy(group, 0, 0, core))

    def serve(group, hop):
        ring_arrived(group, 0, hop)
        if hop < half:
            send(*ring_copy(group, 0, hop))
        send(*sibling_copy(group, 0, hop, core))
        if hop < half:
            ring_arrived(group, 1, hop)
            if hop < half - 1:
                send(*ring_copy(group, 1, hop))
            send(*sibling_copy(group, 1, hop, core))

    def sibling_arrived(group, hop):
        arrived(sibling_copy(group, 0, hop, 1 - core))
        if 0 < hop < half:
            arrived(sibling_copy(group, 1, hop, 1 - core))

    for direction in (0, 1):
        send(*z_copy(direction, 0))
    start_own(0)
    for part in range(CHUNKS):
        for direction in (0, 1):
            send(*coef_copy(direction, 0, part))

    own_queries.wait()
    wide = queries[...].astype(F32)
    norm = jnp.sum(wide * wide, axis=1, keepdims=True)
    high = norm.astype(BF16).astype(F32)
    middle = (norm - high).astype(BF16).astype(F32)
    low = norm - high - middle
    lane = lax.broadcasted_iota(jnp.int32, (n_q, features), 1)
    pieces = jnp.where(lane == 0, high, jnp.where(lane == 1, middle, jnp.where(lane == 2, low, 0.0)))
    wide_queries[:, :features] = (-2.0 * wide).astype(BF16)
    wide_queries[:, features:] = pieces.astype(BF16)
    lane = lax.broadcasted_iota(jnp.int32, ones.shape, 1)
    ones[...] = jnp.where(lane < 3, 1.0, 0.0).astype(BF16)
    own_pattern.wait()

    def piece(slot, hop):
        if hop == half:
            pair = (y, owner_of(0, half))
        else:
            pair = (owner_of(0, hop), owner_of(1, hop))
        listed = pattern[pb, 2 + OFFSETS[slot]].astype(F32)
        top = listed * (5.0 / radius ** 4)
        slope = listed * (4.0 / radius ** 5)
        points = jnp.concatenate(
            [centres[owner * 2 + of_core, slot] for owner in pair for of_core in (0, 1)], axis=0
        )
        point_wide = points.astype(F32)
        square = point_wide * point_wide
        square_high = square.astype(BF16)
        square_low = (square - square_high.astype(F32)).astype(BF16)
        point_norm = lax.dot_general(
            jnp.ones((8, 2 * features), BF16), jnp.concatenate([square_high, square_low], axis=1),
            (((1,), (1,)), ((), ())), preferred_element_type=F32,
        )
        right = jnp.concatenate([points, ones[...]], axis=1)
        tile = n_q // 2

        @pl.loop(0, n_q // tile)
        def _(t):
            span = pl.ds(pl.multiple_of(t * tile, tile), tile)
            cross = lax.dot_general(
                wide_queries[span, :], right, (((1,), (1,)), ((), ())), preferred_element_type=F32
            )
            sq_dist = (cross.reshape(tile // 8, 8, 2 * per_y) + point_norm[None]).reshape(tile, 2 * per_y)
            value = wendland(sq_dist, radius, top, slope)
            for k, owner in enumerate(pair):
                kern[slot, span, pl.ds(pl.multiple_of(owner * per_y, per_y), per_y)] = (
                    value[:, k * per_y:(k + 1) * per_y]
                )

    def compute(group, hop):
        sibling_arrived(group, hop)
        if hop == half:
            sibling_arrived(group, 0)
        for slot in range(*GROUPS[group]):
            piece(slot, hop)

    def coefs_arrived(hop, part, forward):
        for direction in (0, 1):
            arrived(coef_copy(direction, hop, part))
            if forward:
                send(*coef_copy(direction, 1, part))

    def product(slot, first=0, last=CHUNKS):
        span = slice(first * chunk, last * chunk)
        return jnp.dot(kern[slot, :, span], coefs[slot, span, :], preferred_element_type=F32)

    serve(0, 1)
    for direction in (0, 1):
        arrived(z_copy(direction, 0))
        send(*z_copy(direction, 1))
    start_own(1)
    compute(0, 1)
    serve(0, 2)
    serve(1, 1)
    for direction in (0, 1):
        arrived(z_copy(direction, 1))
    start_own(2)
    compute(0, 2)
    serve(0, 3)
    serve(1, 2)
    compute(1, 1)
    serve(2, 1)
    serve(0, 4)
    compute(0, 3)
    serve(1, 3)
    serve(2, 2)
    compute(1, 2)
    serve(1, 4)
    compute(0, 4)
    serve(2, 3)
    total[...] = product(0)
    compute(1, 3)
    serve(2, 4)
    coefs_arrived(0, 0, True)
    coefs_arrived(0, 1, True)
    compute(1, 4)
    compute(2, 1)
    coefs_arrived(0, 2, True)
    compute(2, 2)
    coefs_arrived(0, 3, True)
    compute(2, 3)
    total[...] += product(1) + product(2)
    compute(2, 4)
    for part in range(CHUNKS):
        coefs_arrived(1, part, False)
        partial = product(3, part, part + 1) + product(4, part, part + 1)
        if part < CHUNKS - 1:
            total[...] += partial
        else:
            out_ref[...] = (total[...] + partial).astype(BF16)
    for copy in started:
        copy.wait_send()


def per_device(n_pb, n_ao, queries, centres, coefs, pattern):
    n_q, features = queries.shape
    n_c, columns = coefs.shape
    anywhere = pl.BlockSpec(memory_space=pl.ANY)
    half = n_ao // 4
    dma = pltpu.SemaphoreType.DMA
    return pl.pallas_call(
        functools.partial(kernel, n_pb, n_ao),
        out_shape=jax.ShapeDtypeStruct((n_q, columns), BF16),
        in_specs=[anywhere] * 4,
        out_specs=pl.BlockSpec(memory_space=pltpu.VMEM),
        scratch_shapes=[
            pltpu.VMEM((n_q, features), BF16),
            pltpu.VMEM((n_q, 2 * features), BF16),
            pltpu.VMEM((4 * centres.shape[0], features), BF16),
            pltpu.VMEM((n_ao, 5, centres.shape[0], features), BF16),
            pltpu.VMEM((5, n_c, columns), BF16),
            pltpu.VMEM((5, n_q, n_c), BF16),
            pltpu.VMEM((n_q, columns), F32),
            pltpu.SMEM(pattern.shape, jnp.int32),
            dma((4,)),
            dma((2, 2)), dma((2, 2)),
            dma((3, 2, half)), dma((3, 2, half)),
            dma((3, 2, half + 1)), dma((3, 2, half + 1)),
            dma((2, 2, CHUNKS)), dma((2, 2, CHUNKS)),
        ],
        compiler_params=pltpu.CompilerParams(
            collective_id=0, has_side_effects=True, vmem_limit_bytes=60 * 2 ** 20
        ),
    )(queries, centres, coefs, pattern)


def solution(mesh):
    in_specs = (P("pb", None), P(("pb", "ao"), None), P("pb", "ao"), P())
    out_specs = P("pb", "ao")
    return jax.shard_map(
        functools.partial(per_device, mesh.shape["pb"], mesh.shape["ao"]),
        mesh=mesh, in_specs=in_specs, out_specs=out_specs, check_vma=False,
    )
```

time: 105 us -> 60.9 us (0.58)
  the two profiles are of different devices: /device:TPU:6 before, /device:TPU:1 now
where the time goes in v1:
time: 60.9 us; the launch traced here: 60.7 us
  Pallas kernels  57.5 us (94%)
  local copies, waits for them, and re-layouts  3.24 us (5%)
    pallas_call x1, Pallas kernels, per_device(): pl.pallas_call(functools.partial(kernel, n_pb, n_ao), out_shape=jax.Shape...  57.5 us
    unnamed x2, local copies, waits for them, and re-layouts  3.24 us

profile of v1, /device:TPU:1, one launch (start us, length us, event | category | flops | bytes accessed | tf_op | source)
XLA Modules:
  0.0 60.7 jit_solution(15142620377189173180)
XLA Ops:
  0.0 1.4 %copy.5.pattern_hbm = s32[32,5]{1,0:T(8,128)} copy(s32[32,5]{0,1:T(8,128)} %param.7) | data formatting | bytes 1280 | tf_op args[3]
  1.4 57.5 %shard_map.46 = bf16[1024,256]{1,0:T(8,128)(2,1)} custom-call(bf16[1024,128]{1,0:T(8,128)(2,1)} %queries_hbm.1, bf16[64,128]{1,0:T(8,128)(2,1)} %centres_hbm.1, bf16[1024,256]{1,0:T(8,128)(2,1)} %coefs_hbm.1, s32[32,5]{1,0:T(8,128)} %copy.5.pattern_hbm), custom_call_target="tpu_custom_call" | custom-call | tf_op jit(solution)/shard_map/pallas_call | solution.py:272
  58.8 1.9 %copy.7 = bf16[1024,256]{1,0:T(8,128)(2,1)} copy(bf16[1024,256]{1,0:T(8,128)(2,1)} %shard_map.46) | data formatting | bytes 1048576

commit v2 on v0

v2 whole, which is shorter than its diff:
```python
import functools
import math

import jax
import jax.numpy as jnp
from jax import lax
from jax.experimental import pallas as pl
from jax.experimental.pallas import tpu as pltpu
from jax.sharding import PartitionSpec as P

RADIUS_FACTOR = 1.3
MESH = pl.DeviceIdType.MESH
F32 = jnp.float32
BF16 = jnp.bfloat16

OFFSETS = (0, -1, 1, -2, 2)
GROUPS = ((0, 1), (1, 3), (3, 5))
CHUNKS = 4


def wendland(sq_dist, radius, high, low):
    clamped = jnp.maximum(sq_dist, 1e-30)
    inner = jnp.maximum(radius - clamped * lax.rsqrt(clamped), 0.0)
    square = inner * inner
    return ((square * square) * (high - low * inner)).astype(BF16)


def kernel(
    n_pb, n_ao,
    queries_hbm, centres_hbm, coefs_hbm, pattern_hbm, out_ref,
    queries, wide_queries, ones, centres, coefs, kern, total, pattern,
    local_sem, zs, zr, ys, yr, ss, sr, ks, kr,
):
    n_y = n_ao // 2
    n_q, features = queries.shape
    rows = centres.shape[2]
    block = coefs.shape[1]
    chunk = block // CHUNKS
    share = n_y * rows
    radius = RADIUS_FACTOR * math.sqrt(features)

    pb = lax.axis_index("pb")
    ao = lax.axis_index("ao")
    y = ao // 2
    core = ao % 2
    sibling = (pb, y * 2 + (1 - core))
    steps = sorted(range(1, n_y), key=lambda d: min(d, n_y - d))

    def y_peer(d):
        return (pb, lax.rem(y + d, n_y) * 2 + core)

    def pb_peer(shift):
        return (lax.rem(pb + shift + n_pb, n_pb), ao)

    barrier = pltpu.get_barrier_semaphore()
    peers = [pb_peer(-shift) for shift in OFFSETS[1:]] + [sibling] + [y_peer(d) for d in steps]
    for peer in peers:
        pl.semaphore_signal(barrier, inc=1, device_id=peer, device_id_type=MESH)

    own_centres = pltpu.make_async_copy(centres_hbm, centres.at[y, 0], local_sem.at[0])
    own_coefs = pltpu.make_async_copy(coefs_hbm, coefs.at[0], local_sem.at[1])
    own_queries = pltpu.make_async_copy(queries_hbm, queries, local_sem.at[2])
    own_pattern = pltpu.make_async_copy(pattern_hbm, pattern, local_sem.at[3])
    own_centres.start()
    own_coefs.start()
    own_queries.start()
    own_pattern.start()

    def remote(src, dst, send_sem, recv_sem, device):
        return pltpu.make_async_remote_copy(
            src_ref=src, dst_ref=dst, send_sem=send_sem, recv_sem=recv_sem,
            device_id=device, device_id_type=MESH,
        )

    def z_copy(slot):
        return remote(
            centres.at[y, 0], centres.at[y, slot], zs.at[slot - 1], zr.at[slot - 1],
            pb_peer(-OFFSETS[slot]),
        )

    def coef_copy(direction, hop, part):
        src = 0 if hop == 0 else 1 + direction
        span = pl.ds(part * chunk, chunk)
        return remote(
            coefs.at[src, span], coefs.at[1 + 2 * hop + direction, span],
            ks.at[direction, hop, part], kr.at[direction, hop, part],
            pb_peer(1 if direction == 0 else -1),
        )

    def y_copy(group, d, arriving=False):
        first, last = GROUPS[group]
        owner = lax.rem(y + n_y - d, n_y) if arriving else y
        view = centres.at[owner, pl.ds(first, last - first)]
        return remote(view, view, ys.at[group, d - 1], yr.at[group, d - 1], y_peer(d))

    def kern_copy(slot, arriving=False):
        view = kern.at[1 - core if arriving else core, slot]
        return remote(view, view, ss.at[slot], sr.at[slot], sibling)

    def spread(group):
        for d in steps:
            y_copy(group, d).start()

    def gathered(group):
        for d in steps:
            y_copy(group, d, arriving=True).wait_recv()

    def forward(part):
        for direction in (0, 1):
            coef_copy(direction, 0, part).wait_recv()
            coef_copy(direction, 1, part).start()

    own_centres.wait()
    own_coefs.wait()
    pl.semaphore_wait(barrier, len(peers))

    for slot in range(1, 5):
        z_copy(slot).start()
    for part in range(CHUNKS):
        for direction in (0, 1):
            coef_copy(direction, 0, part).start()
    spread(0)

    own_queries.wait()
    wide = queries[...].astype(F32)
    norm = jnp.sum(wide * wide, axis=1, keepdims=True)
    high = norm.astype(BF16).astype(F32)
    middle = (norm - high).astype(BF16).astype(F32)
    low = norm - high - middle
    lane = lax.broadcasted_iota(jnp.int32, (n_q, features), 1)
    pieces = jnp.where(lane == 0, high, jnp.where(lane == 1, middle, jnp.where(lane == 2, low, 0.0)))
    wide_queries[:, :features] = (-2.0 * wide).astype(BF16)
    wide_queries[:, features:] = pieces.astype(BF16)
    lane = lax.broadcasted_iota(jnp.int32, ones.shape, 1)
    ones[...] = jnp.where(lane < 3, 1.0, 0.0).astype(BF16)
    total[...] = jnp.zeros_like(total)
    own_pattern.wait()

    for group in (1, 2):
        for slot in range(*GROUPS[group]):
            z_copy(slot).wait_recv()
        spread(group)
    gathered(0)

    def evaluate(slot):
        place = 2 + jnp.where(slot % 2 == 1, -1, 1) * ((slot + 1) // 2)
        listed = pattern[place, pb].astype(F32)
        top = listed * (5.0 / radius ** 4)
        slope = listed * (4.0 / radius ** 5)
        points = centres[:, slot].reshape(share, features)
        point_wide = points.astype(F32)
        square = point_wide * point_wide
        square_high = square.astype(BF16)
        square_low = (square - square_high.astype(F32)).astype(BF16)
        point_norm = lax.dot_general(
            jnp.ones((8, 2 * features), BF16), jnp.concatenate([square_high, square_low], axis=1),
            (((1,), (1,)), ((), ())), preferred_element_type=F32,
        )
        right = jnp.concatenate([points, ones[...]], axis=1)
        tile = n_q // 2

        @pl.loop(0, n_q // tile)
        def _(t):
            span = pl.ds(pl.multiple_of(t * tile, tile), tile)
            cross = lax.dot_general(
                wide_queries[span, :], right, (((1,), (1,)), ((), ())), preferred_element_type=F32
            )
            sq_dist = (cross.reshape(tile // 8, 8, share) + point_norm[None]).reshape(tile, share)
            kern[core, slot, span, :] = wendland(sq_dist, radius, top, slope)

    def product(slot, first, n_parts):
        owners = n_y // CHUNKS * n_parts
        start = first * (n_y // CHUNKS)
        columns = pl.ds(pl.multiple_of(start * rows, 128), owners * rows)
        left = jnp.concatenate([kern[c, slot, :, columns] for c in (0, 1)], axis=1)
        right = jnp.concatenate(
            [
                coefs[slot, pl.ds(pl.multiple_of((start + k) * 2 * rows + c * rows, rows), rows), :]
                for c in (0, 1) for k in range(owners)
            ],
            axis=0,
        )
        return jnp.dot(left, right, preferred_element_type=F32)

    @pl.loop(0, 5)
    def _(slot):
        @pl.when(slot == 1)
        def _():
            forward(0)
            gathered(1)
            forward(1)

        @pl.when(slot == 2)
        def _():
            forward(2)

        @pl.when(slot == 3)
        def _():
            forward(3)
            gathered(2)

        evaluate(slot)

        @pl.when(slot > 0)
        def _():
            kern_copy(slot - 1).start()

        @pl.when(slot > 1)
        def _():
            kern_copy(slot - 2, arriving=True).wait_recv()
            total[...] += product(slot - 2, 0, CHUNKS)

    kern_copy(4).start()
    kern_copy(3, arriving=True).wait_recv()
    kern_copy(4, arriving=True).wait_recv()

    @pl.loop(0, CHUNKS)
    def _(part):
        for direction in (0, 1):
            coef_copy(direction, 1, part).wait_recv()
        total[...] += product(3, part, 1) + product(4, part, 1)

    out_ref[...] = total[...].astype(BF16)

    for slot in range(1, 5):
        z_copy(slot).wait_send()
    for group in range(3):
        for d in steps:
            y_copy(group, d).wait_send()
    for part in range(CHUNKS):
        for direction in (0, 1):
            for hop in (0, 1):
                coef_copy(direction, hop, part).wait_send()
    for slot in range(5):
        kern_copy(slot).wait_send()


def per_device(n_pb, n_ao, queries, centres, coefs, pattern):
    n_q, features = queries.shape
    n_c, columns = coefs.shape
    rows = centres.shape[0]
    in_hbm = pl.BlockSpec(memory_space=pltpu.HBM)
    n_y = n_ao // 2
    dma = pltpu.SemaphoreType.DMA
    return pl.pallas_call(
        functools.partial(kernel, n_pb, n_ao),
        out_shape=jax.ShapeDtypeStruct((n_q, columns), BF16),
        in_specs=[in_hbm] * 4,
        out_specs=pl.BlockSpec(memory_space=pltpu.VMEM),
        scratch_shapes=[
            pltpu.VMEM((n_q, features), BF16),
            pltpu.VMEM((n_q, 2 * features), BF16),
            pltpu.VMEM((n_y * rows, features), BF16),
            pltpu.VMEM((n_y, 5, rows, features), BF16),
            pltpu.VMEM((5, n_c, columns), BF16),
            pltpu.VMEM((2, 5, n_q, n_c // 2), BF16),
            pltpu.VMEM((n_q, columns), F32),
            pltpu.SMEM(pattern.shape[::-1], jnp.int32),
            dma((4,)),
            dma((4,)), dma((4,)),
            dma((3, n_y - 1)), dma((3, n_y - 1)),
            dma((5,)), dma((5,)),
            dma((2, 2, CHUNKS)), dma((2, 2, CHUNKS)),
        ],
        compiler_params=pltpu.CompilerParams(
            collective_id=0, has_side_effects=True, vmem_limit_bytes=36 * 2 ** 20
        ),
    )(queries, centres, coefs, pattern.T)


def solution(mesh):
    in_specs = (P("pb", None), P(("pb", "ao"), None), P("pb", "ao"), P())
    out_specs = P("pb", "ao")
    return jax.shard_map(
        functools.partial(per_device, mesh.shape["pb"], mesh.shape["ao"]),
        mesh=mesh, in_specs=in_specs, out_specs=out_specs, check_vma=False,
    )
```

time: 105 us -> 48.2 us (0.46)
  the two profiles are of different devices: /device:TPU:6 before, /device:TPU:1 now
where the time goes in v2:
time: 48.2 us; the launch traced here: 47.9 us
  Pallas kernels  43.7 us (91%)
  local copies, waits for them, and re-layouts  4.19 us (9%)
    pallas_call x1, Pallas kernels, per_device(): pl.pallas_call(functools.partial(kernel, n_pb, n_ao), out_shape=jax.Shape...  43.7 us
    unnamed x9, local copies, waits for them, and re-layouts  4.19 us

profile of v2, /device:TPU:1, one launch (start us, length us, event | category | flops | bytes accessed | tf_op | source)
XLA Modules:
  0.0 47.9 jit_solution(12660824849553089234)
XLA Ops:
  0.0 0.0 copy-start
  0.0 1.0 %copy-done = bf16[1024,256]{1,0:T(8,128)(2,1)S(1)} copy-done((bf16[1024,256]{1,0:T(8,128)(2,1)S(1)}, bf16[1024,256]{1,0:T(8,128)(2,1)}, u32[]{:S(2)}) %copy-start) | copy-done | bytes 524312
  1.0 0.0 copy-start.1
  1.0 0.9 %copy-done.1 = bf16[1024,128]{1,0:T(8,128)(2,1)S(1)} copy-done((bf16[1024,128]{1,0:T(8,128)(2,1)S(1)}, bf16[1024,128]{1,0:T(8,128)(2,1)}, u32[]{:S(2)}) %copy-start.1) | copy-done | bytes 262168
  2.0 0.0 copy-start.2
  2.0 0.7 %copy-done.2 = bf16[64,128]{1,0:T(8,128)(2,1)S(1)} copy-done((bf16[64,128]{1,0:T(8,128)(2,1)S(1)}, bf16[64,128]{1,0:T(8,128)(2,1)}, u32[]{:S(2)}) %copy-start.2) | copy-done | bytes 16408
  2.7 0.0 copy-start.3
  2.7 0.7 %copy-done.3 = s32[32,5]{0,1:T(8,128)S(1)} copy-done((s32[32,5]{0,1:T(8,128)S(1)}, s32[32,5]{0,1:T(8,128)}, u32[]{:S(2)}) %copy-start.3) | copy-done | bytes 664
  3.4 43.7 %shard_map.46 = bf16[1024,256]{1,0:T(8,128)(2,1)S(1)} custom-call(bf16[1024,128]{1,0:T(8,128)(2,1)S(1)} %copy-done.1, bf16[64,128]{1,0:T(8,128)(2,1)S(1)} %copy-done.2, bf16[1024,256]{1,0:T(8,128)(2,1)S(1)} %copy-done, s32[5,32]{1,0:T(8,128)S(1)} %bitcast.1), custom_call_target="tpu_custom_call" | custom-call | tf_op jit(solution)/shard_map/pallas_call | solution.py:245
  47.1 0.8 %copy.6 = bf16[1024,256]{1,0:T(8,128)(2,1)} copy(bf16[1024,256]{1,0:T(8,128)(2,1)S(1)} %shard_map.46) | data formatting | bytes 1048576
Async XLA Ops:
  0.0 1.0 %copy-start = (bf16[1024,256]{1,0:T(8,128)(2,1)S(1)}, bf16[1024,256]{1,0:T(8,128)(2,1)}, u32[]{:S(2)}) copy-start(bf16[1024,256]{1,0:T(8,128)(2,1)} %coefs_hbm.1) | copy-start | bytes 1572868
  1.0 0.9 %copy-start.1 = (bf16[1024,128]{1,0:T(8,128)(2,1)S(1)}, bf16[1024,128]{1,0:T(8,128)(2,1)}, u32[]{:S(2)}) copy-start(bf16[1024,128]{1,0:T(8,128)(2,1)} %queries_hbm.1) | copy-start | bytes 786436
  2.0 0.7 %copy-start.2 = (bf16[64,128]{1,0:T(8,128)(2,1)S(1)}, bf16[64,128]{1,0:T(8,128)(2,1)}, u32[]{:S(2)}) copy-start(bf16[64,128]{1,0:T(8,128)(2,1)} %centres_hbm.1) | copy-start | bytes 49156
  2.7 0.7 %copy-start.3 = (s32[32,5]{0,1:T(8,128)S(1)}, s32[32,5]{0,1:T(8,128)}, u32[]{:S(2)}) copy-start(s32[32,5]{0,1:T(8,128)} %param.7) | copy-start | bytes 1924

commit v3 on v2

--- a/solution.py
+++ b/solution.py
@@ -29,7 +29,7 @@
     n_pb, n_ao,
     queries_hbm, centres_hbm, coefs_hbm, pattern_hbm, out_ref,
     queries, wide_queries, ones, centres, coefs, kern, total, pattern,
-    local_sem, zs, zr, ys, yr, ss, sr, ks, kr,
+    local_sem, ready, far, zs, zr, ys, yr, ss, sr, ks, kr,
 ):
     n_y = n_ao // 2
     n_q, features = queries.shape
@@ -52,10 +52,18 @@
     def pb_peer(shift):
         return (lax.rem(pb + shift + n_pb, n_pb), ao)
 
+    has_below = pb > 0
+    has_above = pb < n_pb - 1
+    sends = (has_above, has_below)
+    receives = (has_below, has_above)
+
     barrier = pltpu.get_barrier_semaphore()
-    peers = [pb_peer(-shift) for shift in OFFSETS[1:]] + [sibling] + [y_peer(d) for d in steps]
-    for peer in peers:
+    for peer in (y_peer(1), y_peer(n_y - 1), sibling):
         pl.semaphore_signal(barrier, inc=1, device_id=peer, device_id_type=MESH)
+
+    @pl.when(has_below)
+    def _():
+        pl.semaphore_signal(barrier, inc=1, device_id=pb_peer(-1), device_id_type=MESH)
 
     own_centres = pltpu.make_async_copy(centres_hbm, centres.at[y, 0], local_sem.at[0])
     own_coefs = pltpu.make_async_copy(coefs_hbm, coefs.at[0], local_sem.at[1])
@@ -72,10 +80,11 @@
             device_id=device, device_id_type=MESH,
         )
 
-    def z_copy(slot):
+    def z_copy(direction, hop):
+        src = 0 if hop == 0 else 1 + direction
         return remote(
-            centres.at[y, 0], centres.at[y, slot], zs.at[slot - 1], zr.at[slot - 1],
-            pb_peer(-OFFSETS[slot]),
+            centres.at[y, src], centres.at[y, 1 + 2 * hop + direction],
+            zs.at[direction, hop], zr.at[direction, hop], pb_peer(1 - 2 * direction),
         )
 
     def coef_copy(direction, hop, part):
@@ -83,8 +92,7 @@
         span = pl.ds(part * chunk, chunk)
         return remote(
             coefs.at[src, span], coefs.at[1 + 2 * hop + direction, span],
-            ks.at[direction, hop, part], kr.at[direction, hop, part],
-            pb_peer(1 if direction == 0 else -1),
+            ks.at[direction, hop, part], kr.at[direction, hop, part], pb_peer(1 - 2 * direction),
         )
 
     def y_copy(group, d, arriving=False):
@@ -108,18 +116,53 @@
     def forward(part):
         for direction in (0, 1):
             coef_copy(direction, 0, part).wait_recv()
-            coef_copy(direction, 1, part).start()
+
+            @pl.when(sends[direction])
+            def _():
+                coef_copy(direction, 1, part).start()
+
+    for direction in (0, 1):
+        @pl.when(jnp.logical_not(receives[direction]))
+        def _():
+            for hop in (0, 1):
+                slot = 1 + 2 * hop + direction
+                pltpu.make_async_copy(centres_hbm, centres.at[y, slot], zr.at[direction, hop]).start()
+                for part in range(CHUNKS):
+                    span = pl.ds(part * chunk, chunk)
+                    pltpu.make_async_copy(
+                        coefs_hbm.at[span], coefs.at[slot, span], kr.at[direction, hop, part]
+                    ).start()
 
     own_centres.wait()
     own_coefs.wait()
-    pl.semaphore_wait(barrier, len(peers))
-
-    for slot in range(1, 5):
-        z_copy(slot).start()
-    for part in range(CHUNKS):
-        for direction in (0, 1):
-            coef_copy(direction, 0, part).start()
-    spread(0)
+    pl.semaphore_wait(barrier, 3 + has_above.astype(jnp.int32))
+
+    @pl.when(has_above)
+    def _():
+        pl.semaphore_signal(ready, inc=1, device_id=pb_peer(1), device_id_type=MESH)
+        z_copy(0, 0).start()
+        for part in range(CHUNKS // 2):
+            coef_copy(0, 0, part).start()
+
+    y_copy(0, 1).start()
+    y_copy(0, n_y - 1).start()
+
+    @pl.when(has_below)
+    def _():
+        pl.semaphore_wait(ready, 1)
+        z_copy(1, 0).start()
+        for part in range(CHUNKS // 2):
+            coef_copy(1, 0, part).start()
+
+    for d in range(2, n_y // 2 + 1):
+        pl.semaphore_signal(far.at[0, d - 2], inc=1, device_id=y_peer(n_y - 1), device_id_type=MESH)
+        if d < n_y - d:
+            pl.semaphore_signal(far.at[1, d - 2], inc=1, device_id=y_peer(1), device_id_type=MESH)
+        pl.semaphore_wait(far.at[0, d - 2], 1)
+        y_copy(0, d).start()
+        if d < n_y - d:
+            pl.semaphore_wait(far.at[1, d - 2], 1)
+            y_copy(0, n_y - d).start()
 
     own_queries.wait()
     wide = queries[...].astype(F32)
@@ -136,10 +179,16 @@
     total[...] = jnp.zeros_like(total)
     own_pattern.wait()
 
-    for group in (1, 2):
-        for slot in range(*GROUPS[group]):
-            z_copy(slot).wait_recv()
-        spread(group)
+    for hop in (0, 1):
+        for direction in (0, 1):
+            z_copy(direction, hop).wait_recv()
+            if hop == 0:
+                @pl.when(sends[direction])
+                def _():
+                    z_copy(direction, 1).start()
+                    for part in range(CHUNKS // 2, CHUNKS):
+                        coef_copy(direction, 0, part).start()
+        spread(hop + 1)
     gathered(0)
 
     def evaluate(slot):
@@ -214,23 +263,28 @@
     kern_copy(3, arriving=True).wait_recv()
     kern_copy(4, arriving=True).wait_recv()
 
-    @pl.loop(0, CHUNKS)
-    def _(part):
+    def last_products(part):
         for direction in (0, 1):
             coef_copy(direction, 1, part).wait_recv()
-        total[...] += product(3, part, 1) + product(4, part, 1)
-
-    out_ref[...] = total[...].astype(BF16)
-
-    for slot in range(1, 5):
-        z_copy(slot).wait_send()
+        return total[...] + (product(3, part, 1) + product(4, part, 1))
+
+    @pl.loop(0, CHUNKS - 1)
+    def _(part):
+        total[...] = last_products(part)
+
+    out_ref[...] = last_products(CHUNKS - 1).astype(BF16)
+
+    for direction in (0, 1):
+        @pl.when(sends[direction])
+        def _():
+            for hop in (0, 1):
+                z_copy(direction, hop).wait_send()
+                for part in range(CHUNKS):
+                    coef_copy(direction, hop, part).wait_send()
+
     for group in range(3):
         for d in steps:
             y_copy(group, d).wait_send()
-    for part in range(CHUNKS):
-        for direction in (0, 1):
-            for hop in (0, 1):
-                coef_copy(direction, hop, part).wait_send()
     for slot in range(5):
         kern_copy(slot).wait_send()
 
@@ -257,7 +311,9 @@
             pltpu.VMEM((n_q, columns), F32),
             pltpu.SMEM(pattern.shape[::-1], jnp.int32),
             dma((4,)),
-            dma((4,)), dma((4,)),
+            pltpu.SemaphoreType.REGULAR,
+            pltpu.SemaphoreType.REGULAR((2, n_y // 2 - 1)),
+            dma((2, 2)), dma((2, 2)),
             dma((3, n_y - 1)), dma((3, n_y - 1)),
             dma((5,)), dma((5,)),
             dma((2, 2, CHUNKS)), dma((2, 2, CHUNKS)),
@@ -265,7 +321,7 @@
         compiler_params=pltpu.CompilerParams(
             collective_id=0, has_side_effects=True, vmem_limit_bytes=36 * 2 ** 20
         ),
-    )(queries, centres, coefs, pattern.T)
+    )(*[pltpu.with_memory_space_constraint(x, pltpu.HBM) for x in (queries, centres, coefs, pattern.T)])
 
 
 def solution(mesh):

time: 48.2 us -> 44.8 us (0.929)
  the two profiles are of different devices: /device:TPU:1 before, /device:TPU:62 now
where the time goes in v3:
time: 44.8 us; the launch traced here: 44.7 us
  Pallas kernels  43.9 us (98%)
  local copies, waits for them, and re-layouts  0.8 us (2%)
    pallas_call x1, Pallas kernels, per_device(): pl.pallas_call(functools.partial(kernel, n_pb, n_ao), out_shape=jax.Shape...  43.9 us

profile of v3, /device:TPU:62, one launch (start us, length us, event | category | flops | bytes accessed | tf_op | source)
XLA Modules:
  0.0 44.7 jit_solution(15414416011248000795)
XLA Ops:
  0.0 43.9 %shard_map.46 = bf16[1024,256]{1,0:T(8,128)(2,1)S(1)} custom-call(bf16[1024,128]{1,0:T(8,128)(2,1)} %queries_hbm.1, bf16[64,128]{1,0:T(8,128)(2,1)} %centres_hbm.1, bf16[1024,256]{1,0:T(8,128)(2,1)} %coefs_hbm.1, s32[5,32]{1,0:T(8,128)} %bitcast.1), custom_call_target="tpu_custom_call" | custom-call | tf_op jit(solution)/shard_map/pallas_call | solution.py:299
  43.9 0.8 %copy.6 = bf16[1024,256]{1,0:T(8,128)(2,1)} copy(bf16[1024,256]{1,0:T(8,128)(2,1)S(1)} %shard_map.46) | data formatting | bytes 1048576

commit v4 on v3

--- a/solution.py
+++ b/solution.py
@@ -14,7 +14,6 @@
 BF16 = jnp.bfloat16
 
 OFFSETS = (0, -1, 1, -2, 2)
-GROUPS = ((0, 1), (1, 3), (3, 5))
 CHUNKS = 4
 
 
@@ -37,6 +36,7 @@
     block = coefs.shape[1]
     chunk = block // CHUNKS
     share = n_y * rows
+    half = n_q // 2
     radius = RADIUS_FACTOR * math.sqrt(features)
 
     pb = lax.axis_index("pb")
@@ -44,8 +44,6 @@
     y = ao // 2
     core = ao % 2
     sibling = (pb, y * 2 + (1 - core))
-    steps = sorted(range(1, n_y), key=lambda d: min(d, n_y - d))
-
     def y_peer(d):
         return (pb, lax.rem(y + d, n_y) * 2 + core)
 
@@ -95,23 +93,42 @@
             ks.at[direction, hop, part], kr.at[direction, hop, part], pb_peer(1 - 2 * direction),
         )
 
-    def y_copy(group, d, arriving=False):
-        first, last = GROUPS[group]
-        owner = lax.rem(y + n_y - d, n_y) if arriving else y
-        view = centres.at[owner, pl.ds(first, last - first)]
-        return remote(view, view, ys.at[group, d - 1], yr.at[group, d - 1], y_peer(d))
-
-    def kern_copy(slot, arriving=False):
-        view = kern.at[1 - core if arriving else core, slot]
-        return remote(view, view, ss.at[slot], sr.at[slot], sibling)
-
-    def spread(group):
-        for d in steps:
-            y_copy(group, d).start()
-
-    def gathered(group):
-        for d in steps:
-            y_copy(group, d, arriving=True).wait_recv()
+    def y_copy(slot, direction, distance, arriving=False):
+        behind = distance if arriving else (0 if distance < 3 else 2)
+        hops = distance if distance < 3 else distance - 2
+        sign = 1 - 2 * direction
+        view = centres.at[lax.rem(y + n_y - sign * behind, n_y), slot]
+        return remote(
+            view, view, ys.at[slot, direction, distance - 1], yr.at[slot, direction, distance - 1],
+            y_peer(n_y + sign * hops),
+        )
+
+    def farthest(slot, direction):
+        return n_y // 2 if direction == slot % 2 else n_y // 2 - 1
+
+    def kern_copy(slot, tile, arriving=False):
+        view = kern.at[1 - core if arriving else core, slot, pl.ds(pl.multiple_of(tile * half, half), half)]
+        return remote(view, view, ss.at[slot, tile], sr.at[slot, tile], sibling)
+
+    def kern_arrived(slot):
+        for tile in (0, 1):
+            kern_copy(slot, tile, arriving=True).wait_recv()
+
+    def spread(slot, distance):
+        for direction in (0, 1):
+            y_copy(slot, direction, distance).start()
+
+    def relay(slot):
+        for direction in (0, 1):
+            y_copy(slot, direction, 2, arriving=True).wait_recv()
+            for distance in range(3, farthest(slot, direction) + 1):
+                y_copy(slot, direction, distance).start()
+
+    def gathered(slot):
+        for direction in (0, 1):
+            for distance in range(1, farthest(slot, direction) + 1):
+                if distance != 2:
+                    y_copy(slot, direction, distance, arriving=True).wait_recv()
 
     def forward(part):
         for direction in (0, 1):
@@ -144,8 +161,11 @@
         for part in range(CHUNKS // 2):
             coef_copy(0, 0, part).start()
 
-    y_copy(0, 1).start()
-    y_copy(0, n_y - 1).start()
+    spread(0, 1)
+    for direction in (0, 1):
+        pl.semaphore_signal(
+            far.at[direction], inc=1, device_id=y_peer(n_y - 1 + 2 * direction), device_id_type=MESH
+        )
 
     @pl.when(has_below)
     def _():
@@ -154,15 +174,9 @@
         for part in range(CHUNKS // 2):
             coef_copy(1, 0, part).start()
 
-    for d in range(2, n_y // 2 + 1):
-        pl.semaphore_signal(far.at[0, d - 2], inc=1, device_id=y_peer(n_y - 1), device_id_type=MESH)
-        if d < n_y - d:
-            pl.semaphore_signal(far.at[1, d - 2], inc=1, device_id=y_peer(1), device_id_type=MESH)
-        pl.semaphore_wait(far.at[0, d - 2], 1)
-        y_copy(0, d).start()
-        if d < n_y - d:
-            pl.semaphore_wait(far.at[1, d - 2], 1)
-            y_copy(0, n_y - d).start()
+    for direction in (0, 1):
+        pl.semaphore_wait(far.at[direction], 1)
+    spread(0, 2)
 
     own_queries.wait()
     wide = queries[...].astype(F32)
@@ -179,16 +193,19 @@
     total[...] = jnp.zeros_like(total)
     own_pattern.wait()
 
-    for hop in (0, 1):
-        for direction in (0, 1):
-            z_copy(direction, hop).wait_recv()
-            if hop == 0:
-                @pl.when(sends[direction])
-                def _():
-                    z_copy(direction, 1).start()
-                    for part in range(CHUNKS // 2, CHUNKS):
-                        coef_copy(direction, 0, part).start()
-        spread(hop + 1)
+    for direction in (0, 1):
+        z_copy(direction, 0).wait_recv()
+
+        @pl.when(sends[direction])
+        def _():
+            z_copy(direction, 1).start()
+            for part in range(CHUNKS // 2, CHUNKS):
+                coef_copy(direction, 0, part).start()
+
+        for distance in (1, 2):
+            spread(1 + direction, distance)
+    for slot in range(3):
+        relay(slot)
     gathered(0)
 
     def evaluate(slot):
@@ -206,16 +223,23 @@
             (((1,), (1,)), ((), ())), preferred_element_type=F32,
         )
         right = jnp.concatenate([points, ones[...]], axis=1)
-        tile = n_q // 2
-
-        @pl.loop(0, n_q // tile)
-        def _(t):
-            span = pl.ds(pl.multiple_of(t * tile, tile), tile)
+
+        @pl.loop(0, 2)
+        def _(tile):
+            span = pl.ds(pl.multiple_of(tile * half, half), half)
             cross = lax.dot_general(
                 wide_queries[span, :], right, (((1,), (1,)), ((), ())), preferred_element_type=F32
             )
-            sq_dist = (cross.reshape(tile // 8, 8, share) + point_norm[None]).reshape(tile, share)
+            sq_dist = (cross.reshape(half // 8, 8, share) + point_norm[None]).reshape(half, share)
             kern[core, slot, span, :] = wendland(sq_dist, radius, top, slope)
+
+            @pl.when(tile == 1)
+            def _():
+                kern_copy(slot, 0).start()
+
+            @pl.when((tile == 0) & (slot > 0))
+            def _():
+                kern_copy(slot - 1, 1).start()
 
     def product(slot, first, n_parts):
         owners = n_y // CHUNKS * n_parts
@@ -231,12 +255,15 @@
         )
         return jnp.dot(left, right, preferred_element_type=F32)
 
-    @pl.loop(0, 5)
+    @pl.loop(0, 6)
     def _(slot):
         @pl.when(slot == 1)
         def _():
             forward(0)
-            gathered(1)
+            for direction in (0, 1):
+                z_copy(direction, 1).wait_recv()
+                for distance in (1, 2):
+                    spread(3 + direction, distance)
             forward(1)
 
         @pl.when(slot == 2)
@@ -245,34 +272,44 @@
 
         @pl.when(slot == 3)
         def _():
+            for late in (3, 4):
+                relay(late)
             forward(3)
-            gathered(2)
-
-        evaluate(slot)
-
-        @pl.when(slot > 0)
-        def _():
-            kern_copy(slot - 1).start()
-
-        @pl.when(slot > 1)
-        def _():
-            kern_copy(slot - 2, arriving=True).wait_recv()
-            total[...] += product(slot - 2, 0, CHUNKS)
-
-    kern_copy(4).start()
-    kern_copy(3, arriving=True).wait_recv()
-    kern_copy(4, arriving=True).wait_recv()
-
-    def last_products(part):
-        for direction in (0, 1):
+
+        @pl.when(slot > 2)
+        def _():
+            kern_arrived(slot - 3)
+            total[...] += product(slot - 3, 0, CHUNKS)
+
+        for k in range(1, 5):
+            @pl.when(slot == k)
+            def _():
+                gathered(k)
+
+        @pl.when(slot < 5)
+        def _():
+            evaluate(slot)
+
+    def far_coefs(direction, parts):
+        for part in parts:
             coef_copy(direction, 1, part).wait_recv()
-        return total[...] + (product(3, part, 1) + product(4, part, 1))
-
-    @pl.loop(0, CHUNKS - 1)
-    def _(part):
-        total[...] = last_products(part)
-
-    out_ref[...] = last_products(CHUNKS - 1).astype(BF16)
+
+    early = CHUNKS // 2
+    kern_copy(4, 1).start()
+    kern_arrived(3)
+    far_coefs(0, range(early))
+    total[...] += product(3, 0, early)
+    kern_arrived(4)
+    far_coefs(1, range(early))
+    total[...] += product(4, 0, early)
+    for part in range(early, CHUNKS):
+        for direction in (0, 1):
+            far_coefs(direction, (part,))
+        partial = product(3, part, 1) + product(4, part, 1)
+        if part < CHUNKS - 1:
+            total[...] += partial
+        else:
+            out_ref[...] = (total[...] + partial).astype(BF16)
 
     for direction in (0, 1):
         @pl.when(sends[direction])
@@ -282,11 +319,13 @@
                 for part in range(CHUNKS):
                     coef_copy(direction, hop, part).wait_send()
 
-    for group in range(3):
-        for d in steps:
-            y_copy(group, d).wait_send()
     for slot in range(5):
-        kern_copy(slot).wait_send()
+        for direction in (0, 1):
+            for distance in range(1, farthest(slot, direction) + 1):
+                y_copy(slot, direction, distance).wait_send()
+    for slot in range(5):
+        for tile in (0, 1):
+            kern_copy(slot, tile).wait_send()
 
 
 def per_device(n_pb, n_ao, queries, centres, coefs, pattern):
@@ -312,10 +351,10 @@
             pltpu.SMEM(pattern.shape[::-1], jnp.int32),
             dma((4,)),
             pltpu.SemaphoreType.REGULAR,
-            pltpu.SemaphoreType.REGULAR((2, n_y // 2 - 1)),
+            pltpu.SemaphoreType.REGULAR((2,)),
             dma((2, 2)), dma((2, 2)),
-            dma((3, n_y - 1)), dma((3, n_y - 1)),
-            dma((5,)), dma((5,)),
+            dma((5, 2, n_y // 2)), dma((5, 2, n_y // 2)),
+            dma((5, 2)), dma((5, 2)),
             dma((2, 2, CHUNKS)), dma((2, 2, CHUNKS)),
         ],
         compiler_params=pltpu.CompilerParams(

time: 44.8 us -> 42 us (0.938)
  the two profiles are of different devices: /device:TPU:62 before, /device:TPU:15 now
where the time goes in v4:
time: 42 us; the launch traced here: 41.9 us
  Pallas kernels  41.1 us (98%)
  local copies, waits for them, and re-layouts  0.8 us (2%)
    pallas_call x1, Pallas kernels, per_device(): pl.pallas_call(functools.partial(kernel, n_pb, n_ao), out_shape=jax.Shape...  41.1 us

profile of v4, /device:TPU:15, one launch (start us, length us, event | category | flops | bytes accessed | tf_op | source)
XLA Modules:
  0.0 41.9 jit_solution(12402431379820058943)
XLA Ops:
  0.0 41.1 %shard_map.46 = bf16[1024,256]{1,0:T(8,128)(2,1)S(1)} custom-call(bf16[1024,128]{1,0:T(8,128)(2,1)} %queries_hbm.1, bf16[64,128]{1,0:T(8,128)(2,1)} %centres_hbm.1, bf16[1024,256]{1,0:T(8,128)(2,1)} %coefs_hbm.1, s32[5,32]{1,0:T(8,128)} %bitcast.1), custom_call_target="tpu_custom_call" | custom-call | tf_op jit(solution)/shard_map/pallas_call | solution.py:338
  41.1 0.8 %copy.6 = bf16[1024,256]{1,0:T(8,128)(2,1)} copy(bf16[1024,256]{1,0:T(8,128)(2,1)S(1)} %shard_map.46) | data formatting | bytes 1048576

commit v5 on v4

--- a/solution.py
+++ b/solution.py
@@ -158,8 +158,7 @@
     def _():
         pl.semaphore_signal(ready, inc=1, device_id=pb_peer(1), device_id_type=MESH)
         z_copy(0, 0).start()
-        for part in range(CHUNKS // 2):
-            coef_copy(0, 0, part).start()
+        coef_copy(0, 0, 0).start()
 
     spread(0, 1)
     for direction in (0, 1):
@@ -171,8 +170,7 @@
     def _():
         pl.semaphore_wait(ready, 1)
         z_copy(1, 0).start()
-        for part in range(CHUNKS // 2):
-            coef_copy(1, 0, part).start()
+        coef_copy(1, 0, 0).start()
 
     for direction in (0, 1):
         pl.semaphore_wait(far.at[direction], 1)
@@ -199,12 +197,17 @@
         @pl.when(sends[direction])
         def _():
             z_copy(direction, 1).start()
-            for part in range(CHUNKS // 2, CHUNKS):
+            for part in range(1, CHUNKS):
                 coef_copy(direction, 0, part).start()
 
         for distance in (1, 2):
             spread(1 + direction, distance)
-    for slot in range(3):
+    relay(0)
+    for direction in (0, 1):
+        z_copy(direction, 1).wait_recv()
+        for distance in (1, 2):
+            spread(3 + direction, distance)
+    for slot in (1, 2):
         relay(slot)
     gathered(0)
 
@@ -260,20 +263,16 @@
         @pl.when(slot == 1)
         def _():
             forward(0)
-            for direction in (0, 1):
-                z_copy(direction, 1).wait_recv()
-                for distance in (1, 2):
-                    spread(3 + direction, distance)
-            forward(1)
-
-        @pl.when(slot == 2)
-        def _():
-            forward(2)
-
-        @pl.when(slot == 3)
-        def _():
             for late in (3, 4):
                 relay(late)
+            forward(1)
+
+        @pl.when(slot == 2)
+        def _():
+            forward(2)
+
+        @pl.when(slot == 3)
+        def _():
             forward(3)
 
         @pl.when(slot > 2)

time: 42 us -> 40.2 us (0.957)
  the two profiles are of different devices: /device:TPU:15 before, /device:TPU:6 now
where the time goes in v5:
time: 40.2 us; the launch traced here: 40 us
  Pallas kernels  39.2 us (98%)
  local copies, waits for them, and re-layouts  0.8 us (2%)
    pallas_call x1, Pallas kernels, per_device(): pl.pallas_call(functools.partial(kernel, n_pb, n_ao), out_shape=jax.Shape...  39.2 us

profile of v5, /device:TPU:6, one launch (start us, length us, event | category | flops | bytes accessed | tf_op | source)
XLA Modules:
  0.0 40.0 jit_solution(4090515499023094588)
XLA Ops:
  0.0 39.2 %shard_map.46 = bf16[1024,256]{1,0:T(8,128)(2,1)S(1)} custom-call(bf16[1024,128]{1,0:T(8,128)(2,1)} %queries_hbm.1, bf16[64,128]{1,0:T(8,128)(2,1)} %centres_hbm.1, bf16[1024,256]{1,0:T(8,128)(2,1)} %coefs_hbm.1, s32[5,32]{1,0:T(8,128)} %bitcast.1), custom_call_target="tpu_custom_call" | custom-call | tf_op jit(solution)/shard_map/pallas_call | solution.py:337
  39.2 0.8 %copy.6 = bf16[1024,256]{1,0:T(8,128)(2,1)} copy(bf16[1024,256]{1,0:T(8,128)(2,1)S(1)} %shard_map.46) | data formatting | bytes 1048576

commit v6 on v5

--- a/solution.py
+++ b/solution.py
@@ -299,16 +299,12 @@
     far_coefs(0, range(early))
     total[...] += product(3, 0, early)
     kern_arrived(4)
-    far_coefs(1, range(early))
-    total[...] += product(4, 0, early)
-    for part in range(early, CHUNKS):
-        for direction in (0, 1):
-            far_coefs(direction, (part,))
-        partial = product(3, part, 1) + product(4, part, 1)
-        if part < CHUNKS - 1:
-            total[...] += partial
-        else:
-            out_ref[...] = (total[...] + partial).astype(BF16)
+    far_coefs(1, range(CHUNKS))
+    total[...] += product(4, 0, CHUNKS)
+    far_coefs(0, range(early, CHUNKS - 1))
+    total[...] += product(3, early, CHUNKS - 1 - early)
+    far_coefs(0, (CHUNKS - 1,))
+    out_ref[...] = (total[...] + product(3, CHUNKS - 1, 1)).astype(BF16)
 
     for direction in (0, 1):
         @pl.when(sends[direction])

time: 40.2 us -> 39.9 us (level)
  no operation moved by 1% of the time
where the time goes in v6:
time: 39.9 us; the launch traced here: 39.7 us
  Pallas kernels  38.9 us (97%)
  local copies, waits for them, and re-layouts  0.8 us (2%)
    pallas_call x1, Pallas kernels, per_device(): pl.pallas_call(functools.partial(kernel, n_pb, n_ao), out_shape=jax.Shape...  38.9 us

profile of v6, /device:TPU:6, one launch (start us, length us, event | category | flops | bytes accessed | tf_op | source)
XLA Modules:
  0.0 39.7 jit_solution(10991870445445900192)
XLA Ops:
  0.0 38.9 %shard_map.46 = bf16[1024,256]{1,0:T(8,128)(2,1)S(1)} custom-call(bf16[1024,128]{1,0:T(8,128)(2,1)} %queries_hbm.1, bf16[64,128]{1,0:T(8,128)(2,1)} %centres_hbm.1, bf16[1024,256]{1,0:T(8,128)(2,1)} %coefs_hbm.1, s32[5,32]{1,0:T(8,128)} %bitcast.1), custom_call_target="tpu_custom_call" | custom-call | tf_op jit(solution)/shard_map/pallas_call | solution.py:333
  38.9 0.8 %copy.6 = bf16[1024,256]{1,0:T(8,128)(2,1)} copy(bf16[1024,256]{1,0:T(8,128)(2,1)S(1)} %shard_map.46) | data formatting | bytes 1048576
